TPU v7x, 32 devices: a whole 2x2x4 slice. The times are simulated.
32 devices in a mesh: seq: 4 (over z), head: 8 (over y, x, core).
Axes of the slice: x: 2, y: 2, z: 4, core: 2. Of those that a mesh axis runs over, the one named last changes fastest.
Arguments:
- query: float32 [3072, 1024], P('seq', 'head'), may hold values from -6 to 6
- key_in: float32 [3072, 1024], P('seq', 'head'), may hold values from -6 to 6
- value: float32 [3072, 1024], P('seq', 'head'), may hold values from -6 to 6
- out_grad: float32 [3072, 1024], P('seq', 'head'), may hold values from -6 to 6
- head_scale: float32 [8], P('head'), may hold values from 0.5 to 2
- norm_gain: float32 [1024], P('head'), may hold values from 0.5 to 1.5
- group_counts: int32 [4], replicated, may hold values from 1 to 6, 12 in all
Outputs:
- normed: float32 [3072, 1024], P('seq', 'head')
- grad_query: float32 [3072, 1024], P('seq', 'head')
- grad_key: float32 [3072, 1024], P('seq', 'head')
- grad_value: float32 [3072, 1024], P('seq', 'head')
Inputs may be any that keep to these rules, and one draw needn't show every extreme that they name: The live rows of shard i are its first 128 * group_counts[i] rows; the counts sum to 3 * 4 and the largest is exactly 6.
All inputs are finite; a program needn't handle non-finite values.
Results may differ from a plain program's by a relative error of at most 0.0001.
Values sent between devices are 32-bit elements; how exact they have to be, the bound alone decides.
A program may use at most 64 MiB of HBM per device.

v0:
```python
import jax
import jax.numpy as jnp
from jax import lax
from jax.sharding import PartitionSpec as P

GROUP = 128


def plain_product(left, right):
    return jnp.dot(left, right, precision=lax.Precision.HIGHEST, preferred_element_type=jnp.float32)


def leading_product(left, right):
    return lax.dot_general(
        left,
        right,
        (((0,), (0,)), ((), ())),
        precision=lax.Precision.HIGHEST,
        preferred_element_type=jnp.float32,
    )


def on_device(query, key_in, value, out_grad, head_scale, norm_gain, group_counts):
    capacity, features_dev = query.shape
    shard_pos = lax.axis_index("seq")
    block_live = group_counts[shard_pos]
    live_rows = (jnp.arange(capacity) < block_live * GROUP)[:, None]
    q_rows = jnp.where(live_rows, query, 0.0)
    k_rows = jnp.where(live_rows, key_in, 0.0)
    v_rows = jnp.where(live_rows, value, 0.0)
    causal = jnp.tril(jnp.ones((GROUP, GROUP), dtype=bool))
    block_total = capacity // GROUP
    zero_state = jnp.zeros((features_dev, features_dev), jnp.float32)

    def forward_step(block_idx, state_pack):
        running, outputs, saved_states, saved_scores = state_pack
        row_start = block_idx * GROUP
        q_block = lax.dynamic_slice_in_dim(q_rows, row_start, GROUP, 0)
        k_block = lax.dynamic_slice_in_dim(k_rows, row_start, GROUP, 0)
        v_block = lax.dynamic_slice_in_dim(v_rows, row_start, GROUP, 0)
        scores = jnp.where(causal, plain_product(q_block, k_block.T), 0.0)
        local_part = plain_product(q_block, running) + plain_product(scores, v_block)
        outputs = lax.dynamic_update_slice_in_dim(outputs, local_part, row_start, 0)
        saved_states = lax.dynamic_update_index_in_dim(saved_states, running, block_idx, 0)
        saved_scores = lax.dynamic_update_index_in_dim(saved_scores, scores, block_idx, 0)
        running = running + leading_product(k_block, v_block)
        return (running, outputs, saved_states, saved_scores)

    forward_init = (
        zero_state,
        jnp.zeros((capacity, features_dev), jnp.float32),
        jnp.zeros((block_total, features_dev, features_dev), jnp.float32),
        jnp.zeros((block_total, GROUP, GROUP), jnp.float32),
    )
    shard_state, local_out, saved_states, saved_scores = lax.fori_loop(
        0, block_live, forward_step, forward_init
    )
    piece_rows = lax.all_gather(shard_state[None], "seq", axis=0, tiled=True)
    picked = (jnp.arange(piece_rows.shape[0]) < shard_pos)[:, None, None]
    state_in = jnp.sum(jnp.where(picked, piece_rows, 0.0), axis=0)
    attended = local_out + plain_product(q_rows, state_in)
    scaled = attended * head_scale[0]
    features = features_dev * lax.axis_size("head")
    squares, cross_terms = lax.psum(
        (jnp.sum(scaled * scaled, axis=1), jnp.sum(norm_gain[None, :] * out_grad * scaled, axis=1)),
        "head",
    )
    inverse = lax.rsqrt(squares / features + 1e-05)[:, None]
    normed = scaled * inverse * norm_gain[None, :]
    grad_scaled = (
        inverse * norm_gain[None, :] * out_grad
        - scaled * inverse * inverse * inverse * cross_terms[:, None] / features
    )
    grad_out = grad_scaled * head_scale[0]

    def backward_step(step_idx, state_pack):
        running, grad_q, grad_k, grad_v = state_pack
        block_idx = block_live - 1 - step_idx
        row_start = block_idx * GROUP
        q_block = lax.dynamic_slice_in_dim(q_rows, row_start, GROUP, 0)
        k_block = lax.dynamic_slice_in_dim(k_rows, row_start, GROUP, 0)
        v_block = lax.dynamic_slice_in_dim(v_rows, row_start, GROUP, 0)
        grad_block = lax.dynamic_slice_in_dim(grad_out, row_start, GROUP, 0)
        held_state = lax.dynamic_index_in_dim(saved_states, block_idx, 0, keepdims=False)
        scores = lax.dynamic_index_in_dim(saved_scores, block_idx, 0, keepdims=False)
        grad_vals = jnp.where(causal, plain_product(grad_block, v_block.T), 0.0)
        query_part = plain_product(grad_block, held_state.T) + plain_product(grad_vals, k_block)
        key_part = leading_product(grad_vals, q_block) + plain_product(v_block, running.T)
        value_part = leading_product(scores, grad_block) + plain_product(k_block, running)
        grad_q = lax.dynamic_update_slice_in_dim(grad_q, query_part, row_start, 0)
        grad_k = lax.dynamic_update_slice_in_dim(grad_k, key_part, row_start, 0)
        grad_v = lax.dynamic_update_slice_in_dim(grad_v, value_part, row_start, 0)
        running = running + leading_product(q_block, grad_block)
        return (running, grad_q, grad_k, grad_v)

    zero_rows = jnp.zeros((capacity, features_dev), jnp.float32)
    shard_grad, grad_q, grad_k, grad_v = lax.fori_loop(
        0, block_live, backward_step, (zero_state, zero_rows, zero_rows, zero_rows)
    )
    piece_rows = lax.all_gather(shard_grad[None], "seq", axis=0, tiled=True)
    picked = (jnp.arange(piece_rows.shape[0]) > shard_pos)[:, None, None]
    state_out = jnp.sum(jnp.where(picked, piece_rows, 0.0), axis=0)
    grad_query = jnp.where(live_rows, grad_q + plain_product(grad_out, state_in.T), 0.0)
    grad_key = jnp.where(live_rows, grad_k + plain_product(v_rows, state_out.T), 0.0)
    grad_value = jnp.where(live_rows, grad_v + plain_product(k_rows, state_out), 0.0)
    return (normed, grad_query, grad_key, grad_value)


def solution(mesh):
    in_specs = (
        P("seq", "head"),
        P("seq", "head"),
        P("seq", "head"),
        P("seq", "head"),
        P("head"),
        P("head"),
        P(),
    )
    out_specs = (P("seq", "head"), P("seq", "head"), P("seq", "head"), P("seq", "head"))
    return jax.shard_map(
        on_device, mesh=mesh, in_specs=in_specs, out_specs=out_specs, check_vma=False
    )
```

profile of v0, /device:TPU:0, one launch (start us, length us, event | category | flops | bytes accessed | tf_op | source)
XLA Modules:
  0.0 91.5 jit_solution(258238342465137067)
XLA Ops:
  0.7 1.2 %copy.12 = f32[768,128]{0,1:T(8,128)S(1)} copy(f32[768,128]{1,0:T(8,128)} %param.14) | data formatting | bytes 786432 | tf_op args[3]
  2.6 0.6 copy-done.6
  3.2 0.7 dynamic_slice.43
  4.6 1.2 %broadcast_select_fusion = (f32[768,128]{1,0:T(8,128)S(1)}, f32[768,128]{1,0:T(8,128)S(1)}, f32[768,128]{1,0:T(8,128)S(1)}) fusion(f32[768,128]{1,0:T(8,128)} %param.11, pred[768]{0:T(1024)(128)(4,1)S(1)} %iota_compare_fusion.2, f32[768,128]{1,0:T(8,128)S(1)} %copy-done, f32[768,128]{1,0:T(8,128)S(1)} %copy-done.1), kind=kLoop, calls=%fused_computation.68 | loop fusion | flops 294912 | bytes 2360064 | tf_op jit(solution)/shard_map/jit(_where)/select_n | solution.py:28
  5.9 4.4 %while.36 = (s32[]{:T(128)}, f32[128,128]{1,0:T(8,128)S(1)}, f32[768,128]{0,1:T(8,128)S(1)}, f32[6,128,128]{2,1,0:T(8,128)S(1)}, f32[6,128,128]{2,1,0:T(8,128)S(...) while((s32[]{:T(128)}, f32[128,128]{1,0:T(8,128)S(1)}, ...), condition=%wide.region_1.2_spmd.clone, body=%wide.region_0.1_spmd.clone.sunk | while | flops 100728832 | bytes 1379053 | solution.py:55
  6.8 0.3 convolution_add_fusion.13
  7.1 0.3 bitcast_dynamic-update-slice_fusion.4
  8.7 0.3 convolution_add_fusion.13
  9.0 0.3 bitcast_dynamic-update-slice_fusion.4
  10.3 20.9 %all-gather = f32[512,128]{1,0:T(8,128)S(1)} all-gather(f32[128,128]{1,0:T(8,128)S(1)} %get-tuple-element.221), channel_id=2, replica_groups=mesh['seq'=4,'head'=8] {'seq'}, dimensions={0}, use_global_device_ids=true | all-gather | bytes 327680 | tf_op jit(solution)/shard_map/all_gather | solution.py:58
  31.3 0.6 copy-done.5
  31.9 0.6 multiply_reduce_fusion
  32.5 12.1 %all-reduce = (f32[768]{0:T(1024)S(1)}, f32[768]{0:T(1024)S(1)}) all-reduce(f32[768]{0:T(1024)S(1)} %get-tuple-element.296, f32[768]{0:T(1024)S(1)} %get-tuple-element.295), channel_id=1, replica_groups=mesh['seq'=4,'head'=8] {'head'}, use_global_device_ids=true, to_apply=%region_4.5 | all-reduce | flops 1536 | bytes 12288 | tf_op jit(solution)/shard_map/psum | solution.py:64
  44.8 0.9 copy.15
  46.5 9.9 %while.37 = (s32[]{:T(128)}, f32[128,128]{1,0:T(8,128)S(1)}, f32[768,128]{1,0:T(8,128)S(1)}, f32[768,128]{1,0:T(8,128)S(1)}, f32[768,128]{1,0:T(8,128)S(1)}, /*i...) while((s32[]{:T(128)}, f32[128,128]{1,0:T(8,128)S(1)}, ...), condition=%wide.region_8.9_spmd.clone, body=%wide.region_7.8_spmd.clone.sunk | while | flops 201424896 | bytes 1840413 | solution.py:97
  47.2 1.1 %fusion.115 = f32[128,128]{1,0:T(8,128)S(1)} fusion(f32[6,128,128]{2,1,0:T(8,128)} %get-tuple-element.581, s32[]{:T(128)S(6)} %select_n.105, f32[768,128]{0,1:T(8,128)S(1)} %get-tuple-element.577, s32[]{:T(128)S(6)} %select_n.104), kind=kOutput, calls=%fused_computation.28.clone.1 | convolution fusion | flops 25165824 | bytes 196616 | tf_op jit(solution)/shard_map/while/body/dot_general | solution.py:14
  48.6 0.3 convolution_select_fusion.3
  48.9 0.3 fusion.113
  49.2 0.3 fusion.114
  49.4 0.3 convolution_add_fusion.15
  49.7 1.1 %fusion.111 = f32[128,128]{1,0:T(8,128)S(1)} fusion(f32[6,128,128]{2,1,0:T(8,128)} %get-tuple-element.578, s32[]{:T(128)S(6)} %select_n.105, f32[768,128]{0,1:T(8,128)S(1)} %get-tuple-element.577, s32[]{:T(128)S(6)} %select_n.104), kind=kOutput, calls=%fused_computation.30.clone.1 | convolution fusion | flops 25165824 | bytes 196616 | tf_op jit(solution)/shard_map/while/body/dot_general | solution.py:10
  51.8 1.1 %fusion.115 = f32[128,128]{1,0:T(8,128)S(1)} fusion(f32[6,128,128]{2,1,0:T(8,128)} %get-tuple-element.581, s32[]{:T(128)S(6)} %select_n.105, f32[768,128]{0,1:T(8,128)S(1)} %get-tuple-element.577, s32[]{:T(128)S(6)} %select_n.104), kind=kOutput, calls=%fused_computation.28.clone.1 | convolution fusion | flops 25165824 | bytes 196616 | tf_op jit(solution)/shard_map/while/body/dot_general | solution.py:14
  53.2 0.3 convolution_select_fusion.3
  53.5 0.3 fusion.113
  53.8 0.3 fusion.114
  54.0 0.3 convolution_add_fusion.15
  54.3 1.1 %fusion.111 = f32[128,128]{1,0:T(8,128)S(1)} fusion(f32[6,128,128]{2,1,0:T(8,128)} %get-tuple-element.578, s32[]{:T(128)S(6)} %select_n.105, f32[768,128]{0,1:T(8,128)S(1)} %get-tuple-element.577, s32[]{:T(128)S(6)} %select_n.104), kind=kOutput, calls=%fused_computation.30.clone.1 | convolution fusion | flops 25165824 | bytes 196616 | tf_op jit(solution)/shard_map/while/body/dot_general | solution.py:10
  55.5 0.2 fusion.112
  56.4 1.5 %fusion.44 = f32[768,128]{1,0:T(8,128)} fusion(f32[768,128]{1,0:T(8,128)S(1)} %get-tuple-element.224, f32[768,128]{0,1:T(8,128)S(1)} %get-tuple-element.587, f32[128,128]{1,0:T(8,128)S(1)} %select_reduce_fusion.1, pred[768]{0:T(1024)(128)(4,1)S(1)} %iota_compare_fusion.2), kind=kOutput, calls=%fused_computation.59 | convolution fusion | flops 151191552 | bytes 1245952 | tf_op jit(solution)/shard_map/dot_general | solution.py:10
  57.9 30.9 %all-gather.1 = f32[512,128]{1,0:T(8,128)S(1)} all-gather(f32[128,128]{1,0:T(8,128)S(1)} %get-tuple-element.226), channel_id=3, replica_groups=mesh['seq'=4,'head'=8] {'seq'}, dimensions={0}, use_global_device_ids=true | all-gather | bytes 327680 | tf_op jit(solution)/shard_map/all_gather | solution.py:100
  88.9 1.3 %fusion.45 = f32[768,128]{1,0:T(8,128)} fusion(f32[768,128]{1,0:T(8,128)S(1)} %get-tuple-element.225, f32[128,128]{1,0:T(8,128)S(1)} %select_reduce_fusion, pred[768]{0:T(1024)(128)(4,1)S(1)} %iota_compare_fusion.2, f32[768,128]{1,0:T(8,128)S(1)} %copy-done), kind=kOutput, calls=%fused_computation.60 | convolution fusion | flops 151289856 | bytes 1245952 | tf_op jit(solution)/shard_map/dot_general | solution.py:10
  90.2 1.3 %fusion.46 = f32[768,128]{1,0:T(8,128)} fusion(f32[768,128]{1,0:T(8,128)S(1)} %get-tuple-element.227, f32[128,128]{1,0:T(8,128)S(1)} %select_reduce_fusion, pred[768]{0:T(1024)(128)(4,1)S(1)} %iota_compare_fusion.2, f32[768,128]{1,0:T(8,128)S(1)} %copy-done.2), kind=kOutput, calls=%fused_computation.61 | convolution fusion | flops 151289856 | bytes 1245952 | tf_op jit(solution)/shard_map/dot_general | solution.py:10
  (40 shorter events, 2.2 us)
Async XLA Ops:
  0.6 3.9 %copy-start = (f32[768,128]{1,0:T(8,128)S(1)}, f32[768,128]{1,0:T(8,128)}, u32[]{:S(2)}) copy-start(f32[768,128]{1,0:T(8,128)} %param.13) | copy-start | bytes 1179652
  0.6 3.9 %copy-start.1 = (f32[768,128]{1,0:T(8,128)S(1)}, f32[768,128]{1,0:T(8,128)}, u32[]{:S(2)}) copy-start(f32[768,128]{1,0:T(8,128)} %param.12) | copy-start | bytes 1179652
  2.5 0.7 copy-start.6
  10.3 20.9 %copy-start.3 = (f32[6,128,128]{2,1,0:T(8,128)}, f32[6,128,128]{2,1,0:T(8,128)S(1)}, u32[]{:S(2)}) copy-start(f32[6,128,128]{2,1,0:T(8,128)S(1)} %get-tuple-element.542) | copy-start | bytes 1179652
  10.3 22.1 %copy-start.4 = (f32[6,128,128]{2,1,0:T(8,128)}, f32[6,128,128]{2,1,0:T(8,128)S(1)}, u32[]{:S(2)}) copy-start(f32[6,128,128]{2,1,0:T(8,128)S(1)} %get-tuple-element.545) | copy-start | bytes 1179652
  31.2 0.7 copy-start.5
  88.9 1.3 %copy-start.2 = (f32[768,128]{1,0:T(8,128)S(1)}, f32[768,128]{1,0:T(8,128)}, u32[]{:S(2)}) copy-start(f32[768,128]{1,0:T(8,128)} %param.12) | copy-start | bytes 1179652
where the time goes:
time: 92.4 us; the launch traced here: 91.5 us
  blocking collectives  63.9 us (69%)
  matrix products  14.3 us (15%)
  loops' own time  4.45 us (5%)
  local copies, waits for them, and re-layouts  4.44 us (5%)
  between operations  2.89 us (3%)
  other arithmetic  1.52 us (2%)
    all_gather x1, blocking collectives, on_device(): piece_rows = lax.all_gather(shard_grad[None], 'seq', axis=0, tiled=True)  30.9 us
    all_gather x1, blocking collectives, on_device(): piece_rows = lax.all_gather(shard_state[None], 'seq', axis=0, tiled=True)  20.9 us
    psum x1, blocking collectives, on_device(): lax.psum((jnp.sum(scaled * scaled, axis=1), jnp.sum(norm_gain[None, :] *...  12.1 us
    dot_general x20, matrix products, plain_product(): jnp.dot(left, right, precision=lax.Precision.HIGHEST, preferred_element_t...  10.3 us
    dot_general x8, matrix products, leading_product(): lax.dot_general(left, right, (((0,), (0,)), ((), ())), precision=lax.Prec...  4 us
    unnamed x16, local copies, waits for them, and re-layouts  3.38 us
    another operation x1, loops' own time, on_device(): lax.fori_loop(0, block_live, backward_step, (zero_state, zero_rows, zero_...  2.23 us
    another operation x1, loops' own time, on_device(): lax.fori_loop(0, block_live, forward_step, forward_init)  2.22 us

commit v1 on v0

--- a/solution.py
+++ b/solution.py
@@ -4,6 +4,19 @@
 from jax.sharding import PartitionSpec as P
 
 GROUP = 128
+
+
+def collect(x, axis, dim):
+    count, index, extent = (lax.axis_size(axis), lax.axis_index(axis), x.shape[dim])
+    forward = [(i, (i + 1) % count) for i in range(count)]
+    out = jnp.zeros((*x.shape[:dim], count * extent, *x.shape[dim + 1 :]), x.dtype)
+    held = x
+    for step in range(count):
+        holder = (index - step) % count
+        out = lax.dynamic_update_slice_in_dim(out, held, holder * extent, axis=dim)
+        if step < count - 1:
+            held = lax.ppermute(held, axis, forward)
+    return out
 
 
 def plain_product(left, right):
@@ -55,7 +68,7 @@
     shard_state, local_out, saved_states, saved_scores = lax.fori_loop(
         0, block_live, forward_step, forward_init
     )
-    piece_rows = lax.all_gather(shard_state[None], "seq", axis=0, tiled=True)
+    piece_rows = collect(shard_state[None], "seq", 0)
     picked = (jnp.arange(piece_rows.shape[0]) < shard_pos)[:, None, None]
     state_in = jnp.sum(jnp.where(picked, piece_rows, 0.0), axis=0)
     attended = local_out + plain_product(q_rows, state_in)

time: 92.4 us -> 84.4 us (0.913)
  blocking collectives: 63.9 us -> 36.2 us
  starting transfers between devices: 0 us -> 13.3 us
  waiting for transfers between devices: 0 us -> 9.51 us
  matrix products: 14.3 us -> 12.6 us
  local copies, waits for them, and re-layouts: 4.44 us -> 3.43 us
    all_gather x1 -> x0, blocking collectives: 20.9 us -> none  [on_device(): piece_rows = lax.all_gather(shard_state[None], 'seq', axis=0, tiled=True)]
    ppermute x0 -> x3, starting transfers between devices: none -> 13.3 us  [collect(): held = lax.ppermute(held, axis, forward)]
    ppermute x0 -> x3, waiting for transfers between devices: none -> 9.51 us  [collect(): held = lax.ppermute(held, axis, forward)]
    all_gather x1, blocking collectives: 30.9 us -> 24.1 us  [on_device(): piece_rows = lax.all_gather(shard_grad[None], 'seq', axis=0, tiled=True)]
    dot_general x20, matrix products: 10.3 us -> 8.62 us  [plain_product(): jnp.dot(left, right, precision=lax.Precision.HIGHEST, preferred_element_t...]
    unnamed x16 -> x14, local copies, waits for them, and re-layouts: 3.38 us -> 2.4 us
  transfers between devices with their start and end apart: 0 -> 3, of which waited for: 0 -> 3; matrix products, arithmetic and copies ran while one was open for 0% -> 0% of each run, Pallas kernels for 0% -> 0%
where the time goes in v1:
time: 84.4 us; the launch traced here: 83.8 us
  blocking collectives  36.2 us (43%)
  starting transfers between devices  13.3 us (16%)
  matrix products  12.6 us (15%)
  waiting for transfers between devices  9.51 us (11%)
  loops' own time  4.24 us (5%)
  local copies, waits for them, and re-layouts  3.43 us (4%)
  between operations  2.83 us (3%)
  other arithmetic  1.75 us (2%)
    all_gather x1, blocking collectives, on_device(): piece_rows = lax.all_gather(shard_grad[None], 'seq', axis=0, tiled=True)  24.1 us
    ppermute x3, starting transfers between devices, collect(): held = lax.ppermute(held, axis, forward)  13.3 us
    psum x1, blocking collectives, on_device(): lax.psum((jnp.sum(scaled * scaled, axis=1), jnp.sum(norm_gain[None, :] *...  12.1 us
    ppermute x3, waiting for transfers between devices, collect(): held = lax.ppermute(held, axis, forward)  9.51 us
    dot_general x20, matrix products, plain_product(): jnp.dot(left, right, precision=lax.Precision.HIGHEST, preferred_element_t...  8.62 us
    dot_general x8, matrix products, leading_product(): lax.dot_general(left, right, (((0,), (0,)), ((), ())), precision=lax.Prec...  4 us
    unnamed x14, local copies, waits for them, and re-layouts  2.4 us
    another operation x1, loops' own time, on_device(): lax.fori_loop(0, block_live, forward_step, forward_init)  2.14 us
  transfers between devices with their start and end apart: 3, of which 3 were waited for; matrix products, arithmetic and copies ran while one was open for 0% of the time, Pallas kernels for 0%

profile of v1, /device:TPU:0, one launch (start us, length us, event | category | flops | bytes accessed | tf_op | source)
XLA Modules:
  0.0 83.8 jit_solution(9700478550802493618)
XLA Ops:
  0.6 0.6 copy-done.5
  1.3 0.6 dynamic_slice.43
  2.5 1.4 %broadcast_select_fusion = (f32[768,128]{1,0:T(8,128)S(1)}, f32[768,128]{1,0:T(8,128)S(1)}, f32[768,128]{1,0:T(8,128)S(1)}) fusion(f32[768,128]{1,0:T(8,128)} %param.11, pred[768]{0:T(1024)(128)(4,1)S(1)} %iota_compare_fusion.2, f32[768,128]{1,0:T(8,128)} %param.13, f32[768,128]{1,0:T(8,128)} %param.12), kind=kLoop, calls=%fused_computation.68 | loop fusion | flops 294912 | bytes 2360064 | tf_op jit(solution)/shard_map/jit(_where)/select_n | solution.py:41
  4.1 4.3 %while.36 = (s32[]{:T(128)}, f32[128,128]{1,0:T(8,128)S(1)}, f32[768,128]{0,1:T(8,128)S(1)}, f32[6,128,128]{2,1,0:T(8,128)S(1)}, f32[6,128,128]{2,1,0:T(8,128)S(...) while((s32[]{:T(128)}, f32[128,128]{1,0:T(8,128)S(1)}, ...), condition=%wide.region_1.2_spmd.clone, body=%wide.region_0.1_spmd.clone.sunk | while | flops 100728832 | bytes 1379053 | solution.py:68
  5.0 0.3 convolution_add_fusion.13
  5.3 0.3 bitcast_dynamic-update-slice_fusion.4
  6.8 0.3 convolution_add_fusion.13
  8.4 10.4 %collective-permute-start = (f32[1,128,128]{2,1,0:T(8,128)S(1)}, f32[1,128,128]{2,1,0:T(8,128)S(1)}, u32[]{:S(2)}, u32[]{:S(2)}) collective-permute-start(f32[1,128,128]{2,1,0:T(8,128)S(1)} %bitcast.49), channel_id=1, source_target_pairs={{0,8},{8,16},{16,24},{24,0},{1,9},{9,17},{17,25},{25,1},{2,10},{10... | collective-permute-start | bytes 196616 | tf_op jit(solution)/shard_map/ppermute | solution.py:18
  20.4 0.3 collective-permute-done
  20.7 2.4 %collective-permute-start.1 = (f32[1,128,128]{2,1,0:T(8,128)S(1)}, f32[1,128,128]{2,1,0:T(8,128)S(1)}, u32[]{:S(2)}, u32[]{:S(2)}) collective-permute-start(f32[1,128,128]{2,1,0:T(8,128)S(1)} %collective-permute-done), channel_id=1, source_target_pairs={{0,8},{8,16},{16,24},{24,0},{1,9},{9,17},{17,25},{25,1},{2,10},{10... | collective-permute-start | bytes 196616 | tf_op jit(solution)/shard_map/ppermute | solution.py:18
  23.1 3.7 %collective-permute-done.1 = f32[1,128,128]{2,1,0:T(8,128)S(1)} collective-permute-done((f32[1,128,128]{2,1,0:T(8,128)S(1)}, f32[1,128,128]{2,1,0:T(8,128)S(1)}, u32[]{:S(2)}, u32[]{:S(2)}) %collective-permute-start.1) | collective-permute-done | bytes 65568 | tf_op jit(solution)/shard_map/ppermute | solution.py:18
  26.7 0.6 collective-permute-start.2
  27.3 5.5 %collective-permute-done.2 = f32[1,128,128]{2,1,0:T(8,128)S(1)} collective-permute-done((f32[1,128,128]{2,1,0:T(8,128)S(1)}, f32[1,128,128]{2,1,0:T(8,128)S(1)}, u32[]{:S(2)}, u32[]{:S(2)}) %collective-permute-start.2) | collective-permute-done | bytes 65568 | tf_op jit(solution)/shard_map/ppermute | solution.py:18
  32.9 0.6 copy-done.4
  33.6 0.6 multiply_reduce_fusion
  34.2 12.1 %all-reduce = (f32[768]{0:T(1024)S(1)}, f32[768]{0:T(1024)S(1)}) all-reduce(f32[768]{0:T(1024)S(1)} %get-tuple-element.296, f32[768]{0:T(1024)S(1)} %get-tuple-element.295), channel_id=1, replica_groups=mesh['seq'=4,'head'=8] {'head'}, use_global_device_ids=true, to_apply=%region_4.5 | all-reduce | flops 1536 | bytes 12288 | tf_op jit(solution)/shard_map/psum | solution.py:77
  46.5 0.9 %copy.15 = f32[768,128]{1,0:T(8,128)} copy(f32[768,128]{0,1:T(8,128)S(1)} %get-tuple-element.346) | data formatting | bytes 786432
  47.5 8.1 %while.37 = (s32[]{:T(128)}, f32[128,128]{1,0:T(8,128)S(1)}, f32[768,128]{1,0:T(8,128)S(1)}, f32[768,128]{1,0:T(8,128)S(1)}, f32[768,128]{1,0:T(8,128)S(1)}, /*i...) while((s32[]{:T(128)}, f32[128,128]{1,0:T(8,128)S(1)}, ...), condition=%wide.region_8.9_spmd.clone, body=%wide.region_7.8_spmd.clone.sunk | while | flops 201424896 | bytes 1840413 | solution.py:110
  48.2 1.1 %fusion.115 = f32[128,128]{1,0:T(8,128)S(1)} fusion(f32[6,128,128]{2,1,0:T(8,128)} %get-tuple-element.581, s32[]{:T(128)S(6)} %select_n.144, f32[768,128]{0,1:T(8,128)S(1)} %get-tuple-element.577, s32[]{:T(128)S(6)} %select_n.143), kind=kOutput, calls=%fused_computation.28.clone.1 | convolution fusion | flops 25165824 | bytes 196616 | tf_op jit(solution)/shard_map/while/body/dot_general | solution.py:27
  49.5 0.3 convolution_select_fusion.3
  49.8 0.3 fusion.113
  50.4 0.3 convolution_add_fusion.15
  50.7 0.3 fusion.111
  51.9 1.1 %fusion.115 = f32[128,128]{1,0:T(8,128)S(1)} fusion(f32[6,128,128]{2,1,0:T(8,128)} %get-tuple-element.581, s32[]{:T(128)S(6)} %select_n.144, f32[768,128]{0,1:T(8,128)S(1)} %get-tuple-element.577, s32[]{:T(128)S(6)} %select_n.143), kind=kOutput, calls=%fused_computation.28.clone.1 | convolution fusion | flops 25165824 | bytes 196616 | tf_op jit(solution)/shard_map/while/body/dot_general | solution.py:27
  53.2 0.3 convolution_select_fusion.3
  53.5 0.3 fusion.113
  54.1 0.3 convolution_add_fusion.15
  54.4 0.3 fusion.111
  55.6 1.5 %fusion.44 = f32[768,128]{1,0:T(8,128)} fusion(f32[768,128]{1,0:T(8,128)S(1)} %get-tuple-element.224, f32[768,128]{0,1:T(8,128)S(1)} %get-tuple-element.588, f32[128,128]{1,0:T(8,128)S(1)} %select_reduce_fusion.1, pred[768]{0:T(1024)(128)(4,1)S(1)} %iota_compare_fusion.2), kind=kOutput, calls=%fused_computation.59 | convolution fusion | flops 151191552 | bytes 1245952 | tf_op jit(solution)/shard_map/dot_general | solution.py:23
  57.1 24.1 %all-gather = f32[512,128]{1,0:T(8,128)S(1)} all-gather(f32[128,128]{1,0:T(8,128)S(1)} %get-tuple-element.226), channel_id=2, replica_groups=mesh['seq'=4,'head'=8] {'seq'}, dimensions={0}, use_global_device_ids=true | all-gather | bytes 327680 | tf_op jit(solution)/shard_map/all_gather | solution.py:113
  81.3 1.3 %fusion.45 = f32[768,128]{1,0:T(8,128)} fusion(f32[768,128]{1,0:T(8,128)S(1)} %get-tuple-element.225, f32[128,128]{1,0:T(8,128)S(1)} %select_reduce_fusion, pred[768]{0:T(1024)(128)(4,1)S(1)} %iota_compare_fusion.2, f32[768,128]{1,0:T(8,128)S(1)} %copy-done), kind=kOutput, calls=%fused_computation.60 | convolution fusion | flops 151289856 | bytes 1245952 | tf_op jit(solution)/shard_map/dot_general | solution.py:23
  82.6 1.3 %fusion.46 = f32[768,128]{1,0:T(8,128)} fusion(f32[768,128]{1,0:T(8,128)S(1)} %get-tuple-element.227, f32[128,128]{1,0:T(8,128)S(1)} %select_reduce_fusion, pred[768]{0:T(1024)(128)(4,1)S(1)} %iota_compare_fusion.2, f32[768,128]{1,0:T(8,128)S(1)} %copy-done.1), kind=kOutput, calls=%fused_computation.61 | convolution fusion | flops 151289856 | bytes 1245952 | tf_op jit(solution)/shard_map/dot_general | solution.py:23
  (48 shorter events, 3.5 us)
Async XLA Ops:
  0.6 0.7 copy-start.5
  4.1 15.4 %copy-start.3 = (f32[768,128]{1,0:T(8,128)S(1)}, f32[768,128]{1,0:T(8,128)}, u32[]{:S(2)}) copy-start(f32[768,128]{1,0:T(8,128)} %param.14) | copy-start | bytes 1179652
  8.4 10.4 %copy-start.2 = (f32[6,128,128]{2,1,0:T(8,128)}, f32[6,128,128]{2,1,0:T(8,128)S(1)}, u32[]{:S(2)}) copy-start(f32[6,128,128]{2,1,0:T(8,128)S(1)} %get-tuple-element.545) | copy-start | bytes 1179652
  8.4 12.3 %collective-permute-start = (f32[1,128,128]{2,1,0:T(8,128)S(1)}, f32[1,128,128]{2,1,0:T(8,128)S(1)}, u32[]{:S(2)}, u32[]{:S(2)}) collective-permute-start(f32[1,128,128]{2,1,0:T(8,128)S(1)} %bitcast.49), channel_id=1, source_target_pairs={{0,8},{8,16},{16,24},{24,0},{1,9},{9,17},{17,25},{25,1},{2,10},{10... | collective-permute-start | bytes 196616 | tf_op jit(solution)/shard_map/ppermute | solution.py:18
  20.7 6.1 %collective-permute-start.1 = (f32[1,128,128]{2,1,0:T(8,128)S(1)}, f32[1,128,128]{2,1,0:T(8,128)S(1)}, u32[]{:S(2)}, u32[]{:S(2)}) collective-permute-start(f32[1,128,128]{2,1,0:T(8,128)S(1)} %collective-permute-done), channel_id=1, source_target_pairs={{0,8},{8,16},{16,24},{24,0},{1,9},{9,17},{17,25},{25,1},{2,10},{10... | collective-permute-start | bytes 196616 | tf_op jit(solution)/shard_map/ppermute | solution.py:18
  26.7 6.1 %collective-permute-start.2 = (f32[1,128,128]{2,1,0:T(8,128)S(1)}, f32[1,128,128]{2,1,0:T(8,128)S(1)}, u32[]{:S(2)}, u32[]{:S(2)}) collective-permute-start(f32[1,128,128]{2,1,0:T(8,128)S(1)} %collective-permute-done.1), channel_id=1, source_target_pairs={{0,8},{8,16},{16,24},{24,0},{1,9},{9,17},{17,25},{25,1},{2,10},{10... | collective-permute-start | bytes 196616 | tf_op jit(solution)/shard_map/ppermute | solution.py:18
  32.9 0.7 copy-start.4
  57.1 24.2 %copy-start = (f32[768,128]{1,0:T(8,128)S(1)}, f32[768,128]{1,0:T(8,128)}, u32[]{:S(2)}) copy-start(f32[768,128]{1,0:T(8,128)} %param.13) | copy-start | bytes 1179652
  81.3 1.3 %copy-start.1 = (f32[768,128]{1,0:T(8,128)S(1)}, f32[768,128]{1,0:T(8,128)}, u32[]{:S(2)}) copy-start(f32[768,128]{1,0:T(8,128)} %param.12) | copy-start | bytes 1179652
